TPU v7x, 128 devices: a whole 4x4x4 slice. The times are simulated.
128 devices in a mesh: rep: 16 (over y, z), grp: 8 (over x, core).
Axes of the slice: x: 4, y: 4, z: 4, core: 2. Of those that a mesh axis runs over, the one named last changes fastest.
Arguments:
- grad_query: float32 [16, 2048, 2048], P('rep', 'grp'), may hold values from -100 to 100, as said below
- error_query: float32 [16, 2048, 2048], P('rep', 'grp'), may hold values from -3 to 3
- basis_query: float32 [2048, 32], replicated, may hold values from -0.125 to 0.125
- momentum_query: float32 [2048, 2048], P('grp'), may hold values from -0.6 to 0.6
- master_query: float32 [2048, 2048], P('grp'), may hold values from -6 to 6
- grad_gate: float32 [16, 2048, 256], P('rep', 'grp'), may hold values from -100 to 100, as said below
- error_gate: float32 [16, 2048, 256], P('rep', 'grp'), may hold values from -3 to 3
- basis_gate: float32 [256, 32], replicated, may hold values from -0.375 to 0.375
- momentum_gate: float32 [2048, 256], P('grp'), may hold values from -0.6 to 0.6
- master_gate: float32 [2048, 256], P('grp'), may hold values from -6 to 6
- vector_grad: float32 [16, 12800], P('rep', 'grp'), may hold values from -6 to 6
- vector_momentum: float32 [12800], P('grp'), may hold values from -0.6 to 0.6
- vector_master: float32 [12800], P('grp'), may hold values from 0.5 to 1.5
Outputs:
- new_error_query: float32 [16, 2048, 2048], P('rep', 'grp')
- new_momentum_query: float32 [2048, 2048], P('grp')
- new_master_query: float32 [2048, 2048], P('grp')
- weight_query: bfloat16 [2048, 2048], replicated
- new_basis_query: float32 [2048, 32], replicated
- new_error_gate: float32 [16, 2048, 256], P('rep', 'grp')
- new_momentum_gate: float32 [2048, 256], P('grp')
- new_master_gate: float32 [2048, 256], P('grp')
- weight_gate: bfloat16 [2048, 256], replicated
- new_basis_gate: float32 [256, 32], replicated
- new_vector_momentum: float32 [12800], P('grp')
- new_vector_master: float32 [12800], P('grp')
- weight_vector: bfloat16 [12800], replicated
Inputs may be any that keep to these rules, and one draw needn't show every extreme that they name: `grad_query`: each replica's gradient is a common part plus a replica's own part. `grad_gate`: each replica's gradient is a common part plus a replica's own part.
All inputs are finite; a program needn't handle non-finite values.
Results may differ from a plain program's by a relative error of at most 0.0006.
Values may be sent and summed in bfloat16 or wider, within the bound.
A program may use at most 128 MiB of HBM per device.

v0:
```python
import jax
import jax.numpy as jnp
from jax import lax
from jax.sharding import PartitionSpec as P

NS_STEPS = 4
highest = lax.Precision.HIGHEST


def inverse_root(gram_matrix):
    trace_value = jnp.trace(gram_matrix)
    identity = jnp.eye(gram_matrix.shape[0], dtype=jnp.float32)
    root_part = gram_matrix / trace_value
    inverse_part = identity
    for iteration in range(NS_STEPS):
        middle = 0.5 * (3.0 * identity - jnp.dot(inverse_part, root_part, precision=highest))
        root_part = jnp.dot(root_part, middle, precision=highest)
        inverse_part = jnp.dot(middle, inverse_part, precision=highest)
    return inverse_part / jnp.sqrt(trace_value)


def right_terms(merged, ortho):
    return jnp.einsum("dn,dr->nr", merged, ortho, precision=highest)


def finish(merged, ortho, new_basis, momentum, master, replicas):
    approx = jnp.dot(ortho, new_basis.T, precision=highest) / replicas
    new_error = (merged - approx)[None]
    new_momentum = 0.9 * momentum + approx
    new_master = master - 0.5 * new_momentum
    return (new_error, new_momentum, new_master)


def per_device(
    grad_query,
    error_query,
    basis_query,
    momentum_query,
    master_query,
    grad_gate,
    error_gate,
    basis_gate,
    momentum_gate,
    master_gate,
    vector_grad,
    vector_momentum,
    vector_master,
):
    replicas = lax.axis_size("rep")
    merged_query = (grad_query + error_query)[0]
    merged_gate = (grad_gate + error_gate)[0]
    local_query = jnp.dot(merged_query, basis_query, precision=highest)
    local_gate = jnp.dot(merged_gate, basis_gate, precision=highest)
    vector_local = vector_grad[0]
    vector_total = lax.psum(vector_local, "rep")
    left_query, left_gate = lax.psum((local_query, local_gate), "rep")
    gram_query, gram_gate = lax.psum(
        (
            jnp.dot(left_query.T, left_query, precision=highest),
            jnp.dot(left_gate.T, left_gate, precision=highest),
        ),
        "grp",
    )
    ortho_query = jnp.dot(left_query, inverse_root(gram_query), precision=highest)
    ortho_gate = jnp.dot(left_gate, inverse_root(gram_gate), precision=highest)
    terms_query = right_terms(merged_query, ortho_query)
    terms_gate = right_terms(merged_gate, ortho_gate)
    basis_new_query, basis_new_gate = lax.psum((terms_query, terms_gate), ("rep", "grp"))
    error_out_query, momentum_out_query, master_out_query = finish(
        merged_query, ortho_query, basis_new_query, momentum_query, master_query, replicas
    )
    error_out_gate, momentum_out_gate, master_out_gate = finish(
        merged_gate, ortho_gate, basis_new_gate, momentum_gate, master_gate, replicas
    )
    vector_mean = vector_total / replicas
    momentum_out_vector = 0.9 * vector_momentum + vector_mean
    master_out_vector = vector_master - 0.5 * momentum_out_vector
    whole_query, whole_gate, whole_vector = (
        lax.all_gather(master_out_query.astype(jnp.bfloat16), "grp", axis=0, tiled=True),
        lax.all_gather(master_out_gate.astype(jnp.bfloat16), "grp", axis=0, tiled=True),
        lax.all_gather(master_out_vector.astype(jnp.bfloat16), "grp", axis=0, tiled=True),
    )
    return (
        error_out_query,
        momentum_out_query,
        master_out_query,
        whole_query,
        basis_new_query,
        error_out_gate,
        momentum_out_gate,
        master_out_gate,
        whole_gate,
        basis_new_gate,
        momentum_out_vector,
        master_out_vector,
        whole_vector,
    )


def solution(mesh):
    in_specs = (
        P("rep", "grp", None),
        P("rep", "grp", None),
        P(),
        P("grp", None),
        P("grp", None),
        P("rep", "grp", None),
        P("rep", "grp", None),
        P(),
        P("grp", None),
        P("grp", None),
        P("rep", "grp"),
        P("grp"),
        P("grp"),
    )
    out_specs = (
        P("rep", "grp", None),
        P("grp", None),
        P("grp", None),
        P(),
        P(),
        P("rep", "grp", None),
        P("grp", None),
        P("grp", None),
        P(),
        P(),
        P("grp"),
        P("grp"),
        P(),
    )
    return jax.shard_map(
        per_device, mesh=mesh, in_specs=in_specs, out_specs=out_specs, check_vma=False
    )
```

profile of v0, /device:TPU:1, one launch (start us, length us, event | category | flops | bytes accessed | tf_op | source)
XLA Modules:
  0.0 369.3 jit_solution(9648238144526546208)
XLA Ops:
  7.2 1.3 reduce
  8.6 4.9 %fusion.2 = f32[256,32]{0,1:T(8,128)} fusion(f32[2048,32]{0,1:T(8,128)S(1)} %copy-done, f32[1,256,2048]{2,1,0:T(8,128)} %param.13, f32[1,256,2048]{2,1,0:T(8,128)} %param.14), kind=kOutput, calls=%fused_computation.4 | convolution fusion | flops 201850880 | bytes 4489216 | tf_op jit(solution)/shard_map/dot_general | solution.py:52
  13.5 1.0 fusion.15
  14.5 0.0 all-reduce.6.cloned.1.call-start
  14.5 83.3 %all-reduce.8.cloned.1.call-done = (f32[256,32]{0,1:T(8,128)}, f32[256,32]{0,1:T(8,128)}, f32[1600]{0:T(1024)}) async-done(((f32[256,32]{0,1:T(8,128)}, f32[256,32]{0,1:T(8,128)}, f32[1600]{0:T(1024)}), (f32[256,32]{0,1:T(8,128)}, f32[256,32]{0,1:T(8,128)}, f32[1600]{0:T(1024)})) %all-reduce.8.cloned.1.call-update) | async-done | bytes 71952 | tf_op jit(solution)/shard_map/psum | solution.py:56
  97.8 1.0 fusion.29
  98.8 1.0 fusion.35
  99.8 22.7 %all-reduce.2 = (f32[32,32]{1,0:T(8,128)S(1)}, f32[32,32]{1,0:T(8,128)S(1)}) all-reduce(f32[32,32]{1,0:T(8,128)S(1)} %fusion.29, f32[32,32]{1,0:T(8,128)S(1)} %fusion.35), channel_id=1, replica_groups=mesh['rep'=16,'grp'=8] {'grp'}, use_global_device_ids=true, to_apply=%region_1.0 | all-reduce | flops 2048 | bytes 16384 | tf_op jit(solution)/shard_map/psum | solution.py:57
  122.5 0.6 select_reduce_fusion
  123.1 0.8 fusion.12
  123.9 0.1 fusion.19
  124.0 0.8 fusion.20
  124.8 0.2 fusion.11
  125.0 0.1 fusion.30
  125.1 0.1 fusion.31
  125.3 0.2 fusion.10
  125.4 0.1 fusion.32
  125.6 0.1 fusion.33
  126.5 0.8 fusion.8
  127.2 0.1 fusion.18
  127.4 0.8 fusion.21
  128.2 0.2 fusion.7
  128.3 0.1 fusion.36
  128.5 0.1 fusion.37
  128.6 0.2 fusion.6
  128.8 0.1 fusion.38
  128.9 0.1 fusion.39
  129.8 0.1 fusion.9
  129.9 0.1 convolution_divide_fusion.1
  130.1 1.0 fusion.34
  131.1 3.8 %fusion = f32[2048,32]{0,1:T(8,128)} fusion(f32[256,32]{0,1:T(8,128)S(1)} %fusion.34, f32[1,256,2048]{2,1,0:T(8,128)S(1)} %copy-done.1, f32[1,256,2048]{2,1,0:T(8,128)} %param.14), kind=kOutput, calls=%fused_computation.2 | convolution fusion | flops 201850880 | bytes 4489216 | tf_op jit(solution)/shard_map/dn,dr->nr/dot_general | solution.py:23
  134.9 0.1 fusion.5
  135.1 0.1 convolution_divide_fusion
  135.3 0.2 fusion.40
  135.5 0.3 fusion.13
  135.8 65.4 %psum.54 = f32[256,32]{0,1:T(8,128)S(1)} all-reduce(f32[256,32]{0,1:T(8,128)S(1)} %fusion.13), channel_id=1, replica_groups=mesh['rep'=16,'grp'=8] {'rep','grp'}, use_global_device_ids=true, to_apply=%region_7.8 | all-reduce | flops 8192 | bytes 65536 | tf_op jit(solution)/shard_map/psum | solution.py:68
  201.2 1.5 fusion.27
  202.7 0.0 all-gather.3.cloned.1.call-start
  202.8 74.1 %all-reduce.6.cloned.1.call-done = f32[2048,32]{0,1:T(8,128)} async-done(((f32[2048,32]{0,1:T(8,128)}), f32[2048,32]{0,1:T(8,128)}) %all-reduce.6.cloned.1.call-update) | async-done | bytes 262160 | tf_op jit(solution)/shard_map/psum | solution.py:68
  276.8 8.2 %fusion.28 = (bf16[256,2048]{1,0:T(8,128)(2,1)}, f32[256,2048]{1,0:T(8,128)}, f32[256,2048]{1,0:T(8,128)}, f32[1,256,2048]{2,1,0:T(8,128)}) fusion(f32[256,2048]{1,0:T(8,128)} %param.17, f32[256,2048]{1,0:T(8,128)} %param.16, f32[1,256,2048]{2,1,0:T(8,128)S(1)} %copy-done.1, f32[1,256,2048]{2,1,0:T(8,128)} %param.14, f32[256,32]{0,1:T(8,128)S(1)} %fusion.34, ...), kind=kOutput, calls=%fused_computation.53 | convolution fusion | flops 205520896 | bytes 16023552 | tf_op jit(solution)/shard_map/dot_general | solution.py:27
  285.1 0.6 dynamic-slice
  286.4 0.6 fusion.26
  287.0 0.2 dynamic-update-slice
  287.3 22.5 %all-reduce = bf16[12800]{0:T(1024)(128)(2,1)} all-reduce(bf16[12800]{0:T(1024)(128)(2,1)S(1)} %dynamic-update-slice), channel_id=1, replica_groups=mesh['rep'=16,'grp'=8] {'grp'}, use_global_device_ids=true, to_apply=%add | all-reduce | flops 12800 | bytes 51200
  309.7 42.8 %all-gather.3.cloned.1.call-done = bf16[2048,2048]{1,0:T(8,128)(2,1)} async-done(((bf16[256,2048]{1,0:T(8,128)(2,1)}), bf16[2048,2048]{1,0:T(8,128)(2,1)}) %all-gather.3.cloned.1.call-update) | async-done | bytes 8388624 | tf_op jit(solution)/shard_map/all_gather | solution.py:79
  352.5 8.5 %copy.33 = bf16[2048,2048]{1,0:T(8,128)(2,1)} copy(bf16[2048,2048]{1,0:T(8,128)(2,1)} %all-gather.3.cloned.1.call-done) | data formatting | bytes 16777216
  361.1 0.7 copy.34
  361.8 1.0 copy.35
  (38 shorter events, 0.2 us)
Async XLA Ops:
  7.2 1.4 copy-start
  7.2 90.6 %all-reduce.8.cloned.1.call-start = ((), (), s32[]{:S(2)}) async-start(), calls=%async_computation.3 | async-start | bytes 147456 | tf_op jit(solution)/shard_map/psum | solution.py:56
  8.6 4.9 %copy-start.2 = (f32[1,256,256]{2,1,0:T(8,128)S(1)}, f32[1,256,256]{2,1,0:T(8,128)}, u32[]{:S(2)}) copy-start(f32[1,256,256]{2,1,0:T(8,128)} %param.18) | copy-start | bytes 786436
  8.6 4.9 %copy-start.3 = (f32[1,256,256]{2,1,0:T(8,128)S(1)}, f32[1,256,256]{2,1,0:T(8,128)}, u32[]{:S(2)}) copy-start(f32[1,256,256]{2,1,0:T(8,128)} %param.19) | copy-start | bytes 786436
  8.6 4.9 %copy-start.10 = (f32[256,32]{0,1:T(8,128)S(1)}, f32[256,32]{0,1:T(8,128)}, u32[]{:S(2)}) copy-start(f32[256,32]{0,1:T(8,128)} %param.20) | copy-start | bytes 98308
  8.6 122.5 %copy-start.1 = (f32[1,256,2048]{2,1,0:T(8,128)S(1)}, f32[1,256,2048]{2,1,0:T(8,128)}, u32[]{:S(2)}) copy-start(f32[1,256,2048]{2,1,0:T(8,128)} %param.13) | copy-start | bytes 6291460
  14.5 262.4 %all-reduce.6.cloned.1.call-start = ((), (), s32[]{:S(2)}) async-start(), calls=%async_computation | async-start | bytes 524288 | tf_op jit(solution)/shard_map/psum | solution.py:68
  131.1 4.2 %copy-start.6 = (f32[256,32]{0,1:T(8,128)S(1)}, f32[256,32]{0,1:T(8,128)}, u32[]{:S(2)}) copy-start(f32[256,32]{0,1:T(8,128)} %get-tuple-element.14) | copy-start | bytes 98308
  131.1 70.1 %copy-start.7 = (f32[256,256]{1,0:T(8,128)S(1)}, f32[256,256]{1,0:T(8,128)}, u32[]{:S(2)}) copy-start(f32[256,256]{1,0:T(8,128)} %param.22) | copy-start | bytes 786436
  131.1 70.1 %copy-start.8 = (f32[256,256]{1,0:T(8,128)S(1)}, f32[256,256]{1,0:T(8,128)}, u32[]{:S(2)}) copy-start(f32[256,256]{1,0:T(8,128)} %param.21) | copy-start | bytes 786436
  134.9 174.8 %all-gather.5.cloned.1.call-start = ((), (), s32[]{:S(2)}) async-start(), calls=%async_computation.2 | async-start | bytes 1179648 | tf_op jit(solution)/shard_map/all_gather | solution.py:80
  201.2 83.9 %copy-start.9 = (f32[256,32]{0,1:T(8,128)}, f32[256,32]{0,1:T(8,128)S(1)}, u32[]{:S(2)}) copy-start(f32[256,32]{0,1:T(8,128)S(1)} %psum.54) | copy-start | bytes 98308
  202.7 82.5 %copy-start.14 = (u32[128]{0:T(128)S(1)}, u32[128]{0:T(128)}, u32[]{:S(2)}) copy-start(u32[128]{0:T(128)} %constant.33) | copy-start | bytes 1540
  202.7 83.7 %copy-start.11 = (f32[1600]{0:T(1024)S(1)}, f32[1600]{0:T(1024)}, u32[]{:S(2)}) copy-start(f32[1600]{0:T(1024)} %param.25) | copy-start | bytes 19204
  202.7 83.7 %copy-start.12 = (f32[1600]{0:T(1024)S(1)}, f32[1600]{0:T(1024)}, u32[]{:S(2)}) copy-start(f32[1600]{0:T(1024)} %param.24) | copy-start | bytes 19204
  202.7 83.7 %copy-start.13 = (f32[1600]{0:T(1024)S(1)}, f32[1600]{0:T(1024)}, u32[]{:S(2)}) copy-start(f32[1600]{0:T(1024)} %get-tuple-element.15) | copy-start | bytes 19204
  202.7 149.8 %all-gather.3.cloned.1.call-start = ((), (), s32[]{:S(2)}) async-start(), calls=%async_computation.1 | async-start | bytes 9437184 | tf_op jit(solution)/shard_map/all_gather | solution.py:79
  352.5 8.6 %copy-start.4 = (f32[2048,32]{0,1:T(8,128)S(1)}, f32[2048,32]{0,1:T(8,128)}, u32[]{:S(2)}) copy-start(f32[2048,32]{0,1:T(8,128)} %all-reduce.6.cloned.1.call-done) | copy-start | bytes 786436
  352.5 9.3 %copy-start.5 = (bf16[2048,256]{1,0:T(8,128)(2,1)S(1)}, bf16[2048,256]{1,0:T(8,128)(2,1)}, u32[]{:S(2)}) copy-start(bf16[2048,256]{1,0:T(8,128)(2,1)} %all-gather.5.cloned.1.call-done) | copy-start | bytes 3145732
Sparse Core Ops, SparseCore 0:
  14.6 83.1 all-reduce.7
  135.0 141.7 all-reduce.5
  279.3 21.1 all-gather.4
  302.7 49.7 all-gather.2
where the time goes:
time: 370 us; the launch traced here: 369 us
  waiting for transfers between devices  200 us (54%)
  blocking collectives  111 us (30%)
  matrix products  28.5 us (8%)
  between operations  16.1 us (4%)
  local copies, waits for them, and re-layouts  11.1 us (3%)
    psum x1, waiting for transfers between devices, per_device(): left_query, left_gate = lax.psum((local_query, local_gate), 'rep')  83.3 us
    psum x1, waiting for transfers between devices, per_device(): lax.psum((terms_query, terms_gate), ('rep', 'grp'))  74.1 us
    psum x1, blocking collectives, per_device(): lax.psum((terms_query, terms_gate), ('rep', 'grp'))  65.4 us
    all_gather x1, waiting for transfers between devices, per_device(): lax.all_gather(master_out_query.astype(jnp.bfloat16), 'grp', axis=0, tile...  42.8 us
    psum x1, blocking collectives, per_device(): lax.psum((jnp.dot(left_query.T, left_query, precision=highest), jnp.dot(l...  22.7 us
    unnamed x1, blocking collectives  22.5 us
    unnamed x36, local copies, waits for them, and re-layouts  11.1 us
    dot_general x2, matrix products, finish(): approx = jnp.dot(ortho, new_basis.T, precision=highest) / replicas  9.7 us
  transfers between devices with their start and end apart: 4, of which 3 were waited for; matrix products, arithmetic and copies ran while one was open for 3% of the time, Pallas kernels for 0%

commit v1 on v0

--- a/solution.py
+++ b/solution.py
@@ -65,7 +65,7 @@
     ortho_gate = jnp.dot(left_gate, inverse_root(gram_gate), precision=highest)
     terms_query = right_terms(merged_query, ortho_query)
     terms_gate = right_terms(merged_gate, ortho_gate)
-    basis_new_query, basis_new_gate = lax.psum((terms_query, terms_gate), ("rep", "grp"))
+    basis_new_query, basis_new_gate = lax.psum(lax.psum((terms_query, terms_gate), "grp"), "rep")
     error_out_query, momentum_out_query, master_out_query = finish(
         merged_query, ortho_query, basis_new_query, momentum_query, master_query, replicas
     )

time: 370 us -> 493 us (1.33)
  waiting for transfers between devices: 200 us -> 265 us
  blocking collectives: 111 us -> 168 us
    psum x1 -> x2, waiting for transfers between devices: 74.1 us -> 144 us  [the longest x1 85.9 us: per_device(): lax.psum(lax.psum((terms_query, terms_gate), 'grp'), 'rep')]
    psum x1 -> x2, blocking collectives: 22.7 us -> 57.5 us  [per_device(): lax.psum((jnp.dot(left_query.T, left_query, precision=highest), jnp.dot(l...]
    psum x1 -> x2, blocking collectives: 65.4 us -> 86.8 us  [the longest x1 62.6 us: per_device(): left_query, left_gate = lax.psum((local_query, local_gate), 'rep')]
    psum x1, waiting for transfers between devices: 83.3 us -> 76.3 us  [per_device(): left_query, left_gate = lax.psum((local_query, local_gate), 'rep')]
    unnamed x36 -> x33, local copies, waits for them, and re-layouts: 11.1 us -> 11.7 us
  transfers between devices with their start and end apart: 4 -> 5, of which waited for: 3 -> 4; matrix products, arithmetic and copies ran while one was open for 3% -> 2% of each run, Pallas kernels for 0% -> 0%
where the time goes in v1:
time: 493 us
  waiting for transfers between devices  265 us (54%)
  blocking collectives  168 us (34%)
  matrix products  28.4 us (6%)
  between operations  16.2 us (3%)
  local copies, waits for them, and re-layouts  11.7 us (2%)
    psum x1, waiting for transfers between devices, per_device(): lax.psum(lax.psum((terms_query, terms_gate), 'grp'), 'rep')  85.9 us
    psum x1, waiting for transfers between devices, per_device(): left_query, left_gate = lax.psum((local_query, local_gate), 'rep')  76.3 us
    psum x1, blocking collectives, per_device(): left_query, left_gate = lax.psum((local_query, local_gate), 'rep')  62.6 us
    psum x1, waiting for transfers between devices, per_device(): lax.psum((terms_query, terms_gate), 'grp')  58 us
    psum x2, blocking collectives, per_device(): lax.psum((jnp.dot(left_query.T, left_query, precision=highest), jnp.dot(l...  57.5 us
    all_gather x1, waiting for transfers between devices, per_device(): lax.all_gather(master_out_query.astype(jnp.bfloat16), 'grp', axis=0, tile...  45 us
    psum x1, blocking collectives, per_device(): lax.psum((terms_query, terms_gate), 'grp')  24.2 us
    unnamed x1, blocking collectives  23.3 us
  transfers between devices with their start and end apart: 5, of which 4 were waited for; matrix products, arithmetic and copies ran while one was open for 2% of the time, Pallas kernels for 0%

profile of v1, /device:TPU:1, one launch (start us, length us, event | category | flops | bytes accessed | tf_op | source)
XLA Modules:
  0.0 492.5 jit_solution(8838899213449355816)
XLA Ops:
  7.2 1.5 fusion.15
  8.8 62.6 %psum.67 = f32[256,32]{0,1:T(8,128)S(1)} all-reduce(f32[256,32]{0,1:T(8,128)S(1)} %fusion.15), channel_id=1, replica_groups=mesh['rep'=16,'grp'=8] {'rep'}, use_global_device_ids=true, to_apply=%region_5.6 | all-reduce | flops 8192 | bytes 65536 | tf_op jit(solution)/shard_map/psum | solution.py:56
  71.4 0.2 fusion.35
  71.6 34.8 %psum.68 = f32[32,32]{1,0:T(8,128)S(1)} all-reduce(f32[32,32]{1,0:T(8,128)S(1)} %fusion.35), channel_id=1, replica_groups=mesh['rep'=16,'grp'=8] {'grp'}, use_global_device_ids=true, to_apply=%region_6.7 | all-reduce | flops 1024 | bytes 8192 | tf_op jit(solution)/shard_map/psum | solution.py:57
  106.4 0.6 select_reduce_fusion
  107.0 0.8 fusion.8
  107.9 0.8 fusion.21
  108.7 0.2 fusion.7
  108.9 0.1 fusion.36
  109.0 0.1 fusion.37
  109.1 0.2 fusion.6
  109.3 0.1 fusion.38
  109.5 0.1 fusion.39
  110.3 0.1 fusion.5
  110.5 0.1 convolution_divide_fusion
  110.6 0.2 fusion.40
  110.9 1.3 fusion.13
  112.2 24.2 %psum.69 = f32[256,32]{0,1:T(8,128)} all-reduce(f32[256,32]{0,1:T(8,128)S(1)} %fusion.13), channel_id=1, replica_groups=mesh['rep'=16,'grp'=8] {'grp'}, use_global_device_ids=true, to_apply=%region_8.9 | all-reduce | flops 8192 | bytes 65536 | tf_op jit(solution)/shard_map/psum | solution.py:68
  136.4 1.3 reduce
  137.7 4.1 fusion.2
  141.8 76.3 %all-reduce.10.cloned.1.call-done = (f32[256,32]{0,1:T(8,128)}, f32[256,32]{0,1:T(8,128)}, f32[1600]{0:T(1024)}) async-done(((f32[256,32]{0,1:T(8,128)}, f32[256,32]{0,1:T(8,128)}, f32[1600]{0:T(1024)}), (f32[256,32]{0,1:T(8,128)}, f32[256,32]{0,1:T(8,128)}, f32[1600]{0:T(1024)})) %all-reduce.10.cloned.1.call-update) | async-done | bytes 71952 | tf_op jit(solution)/shard_map/psum | solution.py:56
  218.1 1.0 fusion.29
  219.1 22.7 %psum.64 = f32[32,32]{1,0:T(8,128)S(1)} all-reduce(f32[32,32]{1,0:T(8,128)S(1)} %fusion.29), channel_id=1, replica_groups=mesh['rep'=16,'grp'=8] {'grp'}, use_global_device_ids=true, to_apply=%region_1.0 | all-reduce | flops 1024 | bytes 8192 | tf_op jit(solution)/shard_map/psum | solution.py:57
  241.8 0.6 select_reduce_fusion.1
  242.4 0.8 fusion.12
  243.3 0.8 fusion.20
  244.1 0.2 fusion.11
  244.3 0.1 fusion.30
  244.4 0.1 fusion.31
  244.6 0.2 fusion.10
  244.8 0.1 fusion.32
  244.9 0.1 fusion.33
  245.9 0.1 convolution_divide_fusion.1
  246.1 1.0 fusion.34
  247.1 3.8 fusion
  251.0 58.0 %all-reduce.6.cloned.1.call-done = f32[2048,32]{0,1:T(8,128)} async-done(((f32[2048,32]{0,1:T(8,128)}), f32[2048,32]{0,1:T(8,128)}) %all-reduce.6.cloned.1.call-update) | async-done | bytes 262160 | tf_op jit(solution)/shard_map/psum | solution.py:68
  309.1 1.4 fusion.27
  310.6 85.9 %all-reduce.8.cloned.1.call-done = f32[2048,32]{0,1:T(8,128)} async-done(((f32[2048,32]{0,1:T(8,128)}), f32[2048,32]{0,1:T(8,128)}) %all-reduce.8.cloned.1.call-update) | async-done | bytes 262160 | tf_op jit(solution)/shard_map/psum | solution.py:68
  396.5 8.2 %fusion.28 = (bf16[256,2048]{1,0:T(8,128)(2,1)}, f32[256,2048]{1,0:T(8,128)}, f32[256,2048]{1,0:T(8,128)}, f32[1,256,2048]{2,1,0:T(8,128)}) fusion(f32[256,2048]{1,0:T(8,128)} %param.17, f32[256,2048]{1,0:T(8,128)} %param.16, f32[1,256,2048]{2,1,0:T(8,128)S(1)} %copy-done.1, f32[1,256,2048]{2,1,0:T(8,128)} %param.14, f32[256,32]{0,1:T(8,128)S(1)} %fusion.34, ...), kind=kOutput, calls=%fused_computation.53 | convolution fusion | flops 205520896 | bytes 16023552 | tf_op jit(solution)/shard_map/dot_general | solution.py:27
  404.8 0.6 dynamic-slice
  406.1 0.6 fusion.26
  406.7 0.2 dynamic-update-slice
  406.9 23.3 %all-reduce = bf16[12800]{0:T(1024)(128)(2,1)} all-reduce(bf16[12800]{0:T(1024)(128)(2,1)S(1)} %dynamic-update-slice), channel_id=1, replica_groups=mesh['rep'=16,'grp'=8] {'grp'}, use_global_device_ids=true, to_apply=%add | all-reduce | flops 12800 | bytes 51200
  430.2 45.0 %all-gather.3.cloned.1.call-done = bf16[2048,2048]{1,0:T(8,128)(2,1)} async-done(((bf16[256,2048]{1,0:T(8,128)(2,1)}), bf16[2048,2048]{1,0:T(8,128)(2,1)}) %all-gather.3.cloned.1.call-update) | async-done | bytes 8388624 | tf_op jit(solution)/shard_map/all_gather | solution.py:79
  475.2 8.5 %copy.34 = bf16[2048,2048]{1,0:T(8,128)(2,1)} copy(bf16[2048,2048]{1,0:T(8,128)(2,1)} %all-gather.3.cloned.1.call-done) | data formatting | bytes 16777216
  483.7 0.7 copy.35
  484.4 1.0 copy.36
  485.4 0.6 copy.37
  (41 shorter events, 0.8 us)
Async XLA Ops:
  7.2 130.5 %copy-start = (f32[2048,32]{0,1:T(8,128)S(1)}, f32[2048,32]{0,1:T(8,128)}, u32[]{:S(2)}) copy-start(f32[2048,32]{0,1:T(8,128)} %param.15) | copy-start | bytes 786436
  7.2 130.5 %copy-start.1 = (f32[1,256,2048]{2,1,0:T(8,128)S(1)}, f32[1,256,2048]{2,1,0:T(8,128)}, u32[]{:S(2)}) copy-start(f32[1,256,2048]{2,1,0:T(8,128)} %param.13) | copy-start | bytes 6291460
  7.2 210.9 %all-reduce.10.cloned.1.call-start = ((), (), s32[]{:S(2)}) async-start(), calls=%async_computation.4 | async-start | bytes 147456 | tf_op jit(solution)/shard_map/psum | solution.py:56
  141.8 167.2 %all-reduce.6.cloned.1.call-start = ((), (), s32[]{:S(2)}) async-start(), calls=%async_computation | async-start | bytes 524288 | tf_op jit(solution)/shard_map/psum | solution.py:68
  247.0 62.0 %copy-start.2 = (f32[1,256,256]{2,1,0:T(8,128)S(1)}, f32[1,256,256]{2,1,0:T(8,128)}, u32[]{:S(2)}) copy-start(f32[1,256,256]{2,1,0:T(8,128)} %param.18) | copy-start | bytes 786436
  247.1 62.0 %copy-start.3 = (f32[1,256,256]{2,1,0:T(8,128)S(1)}, f32[1,256,256]{2,1,0:T(8,128)}, u32[]{:S(2)}) copy-start(f32[1,256,256]{2,1,0:T(8,128)} %param.19) | copy-start | bytes 786436
  247.1 62.0 %copy-start.6 = (f32[256,256]{1,0:T(8,128)S(1)}, f32[256,256]{1,0:T(8,128)}, u32[]{:S(2)}) copy-start(f32[256,256]{1,0:T(8,128)} %param.22) | copy-start | bytes 786436
  247.1 62.0 %copy-start.7 = (f32[256,256]{1,0:T(8,128)S(1)}, f32[256,256]{1,0:T(8,128)}, u32[]{:S(2)}) copy-start(f32[256,256]{1,0:T(8,128)} %param.21) | copy-start | bytes 786436
  247.1 62.0 %copy-start.8 = (f32[256,32]{0,1:T(8,128)S(1)}, f32[256,32]{0,1:T(8,128)}, u32[]{:S(2)}) copy-start(f32[256,32]{0,1:T(8,128)} %get-tuple-element.49) | copy-start | bytes 98308
  250.9 145.6 %all-reduce.8.cloned.1.call-start = ((), (), s32[]{:S(2)}) async-start(), calls=%async_computation.1 | async-start | bytes 524288 | tf_op jit(solution)/shard_map/psum | solution.py:68
  309.0 121.2 %all-gather.5.cloned.1.call-start = ((), (), s32[]{:S(2)}) async-start(), calls=%async_computation.3 | async-start | bytes 1179648 | tf_op jit(solution)/shard_map/all_gather | solution.py:80
  310.5 94.3 %copy-start.12 = (u32[128]{0:T(128)S(1)}, u32[128]{0:T(128)}, u32[]{:S(2)}) copy-start(u32[128]{0:T(128)} %constant.33) | copy-start | bytes 1540
  310.5 95.5 %copy-start.9 = (f32[1600]{0:T(1024)S(1)}, f32[1600]{0:T(1024)}, u32[]{:S(2)}) copy-start(f32[1600]{0:T(1024)} %param.25) | copy-start | bytes 19204
  310.5 95.5 %copy-start.10 = (f32[1600]{0:T(1024)S(1)}, f32[1600]{0:T(1024)}, u32[]{:S(2)}) copy-start(f32[1600]{0:T(1024)} %param.24) | copy-start | bytes 19204
  310.5 95.5 %copy-start.11 = (f32[1600]{0:T(1024)S(1)}, f32[1600]{0:T(1024)}, u32[]{:S(2)}) copy-start(f32[1600]{0:T(1024)} %get-tuple-element.15) | copy-start | bytes 19204
  310.5 164.6 %all-gather.3.cloned.1.call-start = ((), (), s32[]{:S(2)}) async-start(), calls=%async_computation.2 | async-start | bytes 9437184 | tf_op jit(solution)/shard_map/all_gather | solution.py:79
  475.2 8.6 %copy-start.4 = (f32[2048,32]{0,1:T(8,128)S(1)}, f32[2048,32]{0,1:T(8,128)}, u32[]{:S(2)}) copy-start(f32[2048,32]{0,1:T(8,128)} %all-reduce.8.cloned.1.call-done) | copy-start | bytes 786436
  475.2 9.3 %copy-start.5 = (bf16[2048,256]{1,0:T(8,128)(2,1)S(1)}, bf16[2048,256]{1,0:T(8,128)(2,1)}, u32[]{:S(2)}) copy-start(bf16[2048,256]{1,0:T(8,128)(2,1)} %all-gather.5.cloned.1.call-done) | copy-start | bytes 3145732
Sparse Core Ops, SparseCore 0:
  141.9 76.2 all-reduce.9
  251.0 57.9 all-reduce.5
  312.2 84.3 all-reduce.7
  398.8 24.3 all-gather.4
  425.4 49.7 all-gather.2
